TPU v7x, 256 devices: a whole 4x4x8 slice. The times are simulated.
256 devices in a mesh: member: 16 (over x, y_lo, core), sub: 16 (over y_hi, z).
Axes of the slice: x: 4, y: 4 (y_hi: 2, y_lo: 2; y = y_hi * 2 + y_lo), z: 8, core: 2. Of those that a mesh axis runs over, the one named last changes fastest.
Arguments:
- velocity: float32 [16, 3, 256, 32, 128], P('member', None, 'sub'), may hold values from -8 to 8
- forcing: float32 [16, 3, 256, 32, 128], P('member', None, 'sub'), may hold values from -16 to 16
Outputs:
- new_velocity: float32 [16, 3, 256, 32, 128], P('member', None, 'sub')
All inputs are finite; a program needn't handle non-finite values.
Results may differ from a plain program's by a relative error of at most 0.00029.
Values sent between devices are 32-bit elements; how exact they have to be, the bound alone decides.
A program may use at most 64 MiB of HBM per device.

v0:
```python
import math

import jax
import jax.numpy as jnp
from jax import lax
from jax.sharding import PartitionSpec as P

SWEEPS = 8


TIME_STEP = 0.25
EDDY_COEFF = 1.0
BASE_VISCOSITY = 1.0
LOWER_EDGE = 0.1
UPPER_EDGE = 1.9


def with_halo(block, sides, width):
    for axis, dim in sides:
        count = lax.axis_size(axis)
        forward = [(i, i + 1) for i in range(count - 1)]
        forward.append((count - 1, 0))
        backward = [(target, source) for source, target in forward]
        low = lax.ppermute(
            lax.slice_in_dim(block, block.shape[dim] - width, None, axis=dim), axis, forward
        )
        high = lax.ppermute(lax.slice_in_dim(block, 0, width, axis=dim), axis, backward)
        block = jnp.concatenate([low, block, high], axis=dim)
    return block


def cut_along(array, dim, devices):
    before, after = (array.shape[:dim], array.shape[dim + 1 :])
    return jnp.moveaxis(array.reshape(*before, devices, -1, *after), dim, 0)


def summed_on_arrival(array, axis, dim):
    devices = lax.axis_size(axis)
    tiles = lax.all_to_all(cut_along(array, dim, devices), axis, 0, 0, tiled=True)
    return jnp.sum(tiles, axis=0)


def sent_to_all(array, axis):
    copies = jnp.broadcast_to(array, (lax.axis_size(axis), *array.shape))
    return lax.all_to_all(copies, axis, split_axis=0, concat_axis=0, tiled=True)


def joined_along(tiles, dim):
    tiles = jnp.moveaxis(tiles, 0, dim)
    dims = tiles.shape
    return tiles.reshape(*dims[:dim], dims[dim] * dims[dim + 1], *dims[dim + 2 :])


def collect(array, axis, dim):
    tiles = sent_to_all(array, axis)
    return joined_along(tiles, dim)


def step_sizes(sweep_count):
    middle = (UPPER_EDGE + LOWER_EDGE) / 2
    radius = (UPPER_EDGE - LOWER_EDGE) / 2
    return [
        1.0 / (middle + radius * math.cos(math.pi * (2 * position + 1) / (2 * sweep_count)))
        for position in range(sweep_count)
    ]


def trimmed(array, amount, axis_number):
    if amount == 0:
        return array
    return lax.slice_in_dim(array, amount, array.shape[axis_number] - amount, axis=axis_number)


def coefficients(visc_ext):
    center = visc_ext[1:-1]
    east_face = 0.5 * (center + visc_ext[2:])
    west_face = 0.5 * (center + visc_ext[:-2])
    north_face = 0.5 * (center + jnp.roll(center, -1, 1))
    south_face = 0.5 * (center + jnp.roll(center, 1, 1))
    upper_face = 0.5 * (center + jnp.roll(center, -1, 2))
    lower_face = 0.5 * (center + jnp.roll(center, 1, 2))
    diagonal = 1.0 + TIME_STEP * (
        east_face + west_face + north_face + south_face + upper_face + lower_face
    )
    return (east_face, west_face, north_face, south_face, upper_face, lower_face, diagonal)


def sweep(field, rim_width, coeffs, coeff_rim, source, source_rim, step_size):
    cut = [trimmed(entry, coeff_rim - (rim_width - 1), 0) for entry in coeffs]
    east_face, west_face, north_face, south_face, upper_face, lower_face, diagonal = cut
    center = field[:, 1:-1]
    neighbours = east_face * field[:, 2:] + west_face * field[:, :-2]
    neighbours = (
        neighbours + north_face * jnp.roll(center, -1, 2) + south_face * jnp.roll(center, 1, 2)
    )
    neighbours = (
        neighbours + upper_face * jnp.roll(center, -1, 3) + lower_face * jnp.roll(center, 1, 3)
    )
    image = diagonal * center - TIME_STEP * neighbours
    local_source = trimmed(source, source_rim - (rim_width - 1), 1)
    return center + step_size * (local_source - image) / diagonal


def relax_group(field, depth, coeffs, coeff_rim, source, source_rim, group_sizes):
    for offset, step_size in enumerate(group_sizes):
        field = sweep(field, depth - offset, coeffs, coeff_rim, source, source_rim, step_size)
    return field


def per_device(velocity, forcing):
    members = lax.axis_size("member")
    flow = velocity[0]
    member_force = forcing[0]
    flow_ext = with_halo(flow, (("sub", 1),), 1)
    differences = [
        (flow_ext[:, 2:] - flow_ext[:, :-2]) * 0.5,
        (jnp.roll(flow, -1, 2) - jnp.roll(flow, 1, 2)) * 0.5,
        (jnp.roll(flow, -1, 3) - jnp.roll(flow, 1, 3)) * 0.5,
    ]
    stacked = jnp.concatenate([flow, jnp.sum(flow * flow, 0)[None]], 0).reshape(4, -1)
    shares = summed_on_arrival(stacked, "member", 1)
    mean_share = shares[:3] / members
    spread_share = shares[3] / members - jnp.sum(mean_share * mean_share, 0)
    visc_share = BASE_VISCOSITY + EDDY_COEFF * TIME_STEP * spread_share
    joined = collect(jnp.concatenate([mean_share, visc_share[None]], 0), "member", 1)
    joined = joined.reshape((4,) + flow.shape[1:])
    mean_flow = joined[:3]
    viscosity = joined[3]
    transport = (
        mean_flow[0] * differences[0]
        + mean_flow[1] * differences[1]
        + mean_flow[2] * differences[2]
    )
    source = flow - TIME_STEP * transport + TIME_STEP * member_force
    sizes_list = step_sizes(SWEEPS)
    field = source
    visc_ext = with_halo(viscosity, (("sub", 0),), 5)
    coeffs = coefficients(visc_ext)
    source_ext = with_halo(source, (("sub", 1),), 3)
    for group_number in range(SWEEPS // 4):
        extended = with_halo(field, (("sub", 1),), 4)
        field = relax_group(
            extended,
            4,
            coeffs,
            4,
            source_ext,
            3,
            sizes_list[4 * group_number : 4 * group_number + 4],
        )
    return field[None]


def solution(mesh):
    in_specs = (P("member", None, "sub", None, None), P("member", None, "sub", None, None))
    out_specs = P("member", None, "sub", None, None)
    return jax.shard_map(
        per_device, mesh=mesh, in_specs=in_specs, out_specs=out_specs, check_vma=False
    )
```

profile of v0, /device:TPU:1, one launch (start us, length us, event | category | flops | bytes accessed | tf_op | source)
XLA Modules:
  0.0 100.5 jit_solution(10576627885520325677)
XLA Ops:
  0.0 1.3 %multiply_reduce_fusion = f32[16,32,128]{2,1,0:T(8,128)S(1)} fusion(f32[1,3,16,32,128]{4,3,2,1,0:T(8,128)} %param.2), kind=kLoop, calls=%fused_computation.165 | loop fusion | flops 327680 | bytes 1048576 | tf_op jit(solution)/shard_map/reduce_sum | solution.py:120
  1.4 0.1 concatenate.172
  1.6 0.1 maximum_bitcast_fusion
  1.7 1.7 %copy.4 = f32[16,4,4096]{2,1,0:T(4,128)} copy(f32[16,4,4096]{2,0,1:T(8,128)S(1)} %maximum_bitcast_fusion) | data formatting | bytes 2097152 | tf_op jit(solution)/shard_map/transpose | solution.py:34
  3.3 6.8 %all-to-all-start = ((f32[16,4,4096]{2,1,0:T(4,128)}), f32[16,4,4096]{2,1,0:T(4,128)S(1)}, u32[]{:S(2)}, u32[]{:S(2)}) async-start(f32[16,4,4096]{2,1,0:T(4,128)} %copy.4), calls=%async_computation | async-start | bytes 2097152 | tf_op jit(solution)/shard_map/all_to_all | solution.py:39
  10.1 0.6 fusion.162
  10.8 7.9 %collective-permute-start = (f32[3,1,32,128]{3,2,1,0:T(8,128)}, f32[3,1,32,128]{3,2,1,0:T(8,128)S(1)}, u32[]{:S(2)}, u32[]{:S(2)}) collective-permute-start(f32[3,1,32,128]{3,2,1,0:T(8,128)} %get-tuple-element.92), channel_id=1, source_target_pairs={{1,0},{2,1},{3,2},{4,3},{5,4},{6,5},{7,6},{8,7},{9,8},{10,9},{11,1... | collective-permute-start | bytes 147464 | tf_op jit(solution)/shard_map/ppermute | solution.py:27
  18.7 7.3 %all-to-all-done = f32[16,4,4096]{2,1,0:T(4,128)S(1)} async-done(((f32[16,4,4096]{2,1,0:T(4,128)}), f32[16,4,4096]{2,1,0:T(4,128)S(1)}, u32[]{:S(2)}, u32[]{:S(2)}) %all-to-all-start) | async-done | bytes 1048608 | tf_op jit(solution)/shard_map/all_to_all | solution.py:39
  26.0 0.2 reduce_sum.30
  26.3 1.2 %broadcast_in_dim.4 = f32[16,4,4096]{2,1,0:T(4,128)} broadcast(f32[4,4096]{1,0:T(4,128)S(1)} %pad_maximum_fusion.18), dimensions={1,2} | broadcast | bytes 1114112 | tf_op jit(solution)/shard_map/broadcast_in_dim | solution.py:44
  27.5 4.7 %all-to-all-start.1 = ((f32[16,4,4096]{2,1,0:T(4,128)}), f32[16,4,4096]{2,1,0:T(4,128)S(1)}, u32[]{:S(2)}, u32[]{:S(2)}) async-start(f32[16,4,4096]{2,1,0:T(4,128)} %broadcast_in_dim.4), calls=%async_computation.1 | async-start | bytes 2097152 | tf_op jit(solution)/shard_map/all_to_all | solution.py:45
  32.3 0.3 fusion.158
  32.6 1.4 %fusion.159 = (f32[3,16,32,127]{3,2,1,0:T(8,128)}, f32[3,16,32,127]{3,2,1,0:T(8,128)}) fusion(f32[3,16,32,128]{3,2,1,0:T(8,128)S(1)} %bitcast.21), kind=kLoop, calls=%fused_computation.232 | loop fusion | bytes 3121152 | tf_op jit(solution)/shard_map/jit(_roll_static)/slice | solution.py:118
  34.0 1.3 %fusion.161 = (f32[3,16,31,128]{3,2,1,0:T(8,128)}, f32[3,16,31,128]{3,2,1,0:T(8,128)}) fusion(f32[3,16,32,128]{3,2,1,0:T(8,128)S(1)} %bitcast.22), kind=kLoop, calls=%fused_computation.234 | loop fusion | bytes 3047424 | tf_op jit(solution)/shard_map/jit(_roll_static)/slice | solution.py:117
  35.3 12.5 %all-to-all-done.1 = f32[16,4,4096]{2,1,0:T(4,128)S(1)} async-done(((f32[16,4,4096]{2,1,0:T(4,128)}), f32[16,4,4096]{2,1,0:T(4,128)S(1)}, u32[]{:S(2)}, u32[]{:S(2)}) %all-to-all-start.1) | async-done | bytes 1048608 | tf_op jit(solution)/shard_map/all_to_all | solution.py:45
  47.8 1.2 %fusion.138 = (f32[1,16,4096]{2,0,1:T(1,128)S(1)}, f32[1,16,4096]{2,0,1:T(1,128)S(1)}, f32[1,16,4096]{2,0,1:T(1,128)S(1)}, f32[1,16,4096]{2,0,1:T(1,128)S(1)}) fusion(f32[4,16,4096]{2,0,1:T(4,128)S(1)} %bitcast.24), kind=kLoop, calls=%fused_computation.211 | loop fusion | flops 196608 | bytes 2097152 | tf_op jit(solution)/shard_map/slice | solution.py:128
  49.0 0.2 fusion.137
  49.2 7.4 %collective-permute-start.7 = (f32[5,32,128]{2,1,0:T(8,128)S(1)}, f32[5,32,128]{2,1,0:T(8,128)S(1)}, u32[]{:S(2)}, u32[]{:S(2)}) collective-permute-start(f32[5,32,128]{2,1,0:T(8,128)S(1)} %bitcast.32), channel_id=1, source_target_pairs={{1,0},{2,1},{3,2},{4,3},{5,4},{6,5},{7,6},{8,7},{9,8},{10,9},{11,1... | collective-permute-start | bytes 245768 | tf_op jit(solution)/shard_map/ppermute | solution.py:27
  56.6 2.3 %fusion.102 = f32[3,16,32,128]{3,2,1,0:T(8,128)S(1)} fusion(f32[3,16,32,128]{3,2,1,0:T(8,128)S(1)} %bitcast.23, f32[3,1,32,128]{3,2,1,0:T(8,128)S(1)} %collective-permute-done.1, f32[3,1,32,128]{3,2,1,0:T(8,128)S(1)} %collective-permute-done, f32[3,16,1,128]{3,2,1,0:T(1,128)S(1)} %get-tuple-element.89, f32[3,16,31,128]{3,2,1,0:T(8,128)} %get-tuple-element.91, ...), kind=kLoop, calls=%fused_computation.151 | loop fusion | flops 3538944 | bytes 6389760 | tf_op jit(solution)/shard_map/add | solution.py:134
  59.0 0.1 collective-permute-start.4
  59.1 5.1 %collective-permute-start.5 = (f32[3,3,32,128]{3,2,1,0:T(8,128)S(1)}, f32[3,3,32,128]{3,2,1,0:T(8,128)S(1)}, u32[]{:S(2)}, u32[]{:S(2)}) collective-permute-start(f32[3,3,32,128]{3,2,1,0:T(8,128)S(1)} %get-tuple-element.81), channel_id=1, source_target_pairs={{1,0},{2,1},{3,2},{4,3},{5,4},{6,5},{7,6},{8,7},{9,8},{10,9},{11,1... | collective-permute-start | bytes 442376 | tf_op jit(solution)/shard_map/ppermute | solution.py:27
  64.2 5.1 %collective-permute-start.3 = (f32[3,4,32,128]{3,2,1,0:T(8,128)S(1)}, f32[3,4,32,128]{3,2,1,0:T(8,128)S(1)}, u32[]{:S(2)}, u32[]{:S(2)}) collective-permute-start(f32[3,4,32,128]{3,2,1,0:T(8,128)S(1)} %get-tuple-element.83), channel_id=1, source_target_pairs={{1,0},{2,1},{3,2},{4,3},{5,4},{6,5},{7,6},{8,7},{9,8},{10,9},{11,1... | collective-permute-start | bytes 589832 | tf_op jit(solution)/shard_map/ppermute | solution.py:27
  69.3 0.2 fusion.164
  69.5 0.2 fusion.163
  69.8 0.5 multiply_add_fusion
  71.2 0.1 pad_maximum_fusion.10
  71.2 1.1 %collective-permute-done.2 = f32[3,4,32,128]{3,2,1,0:T(8,128)S(1)} collective-permute-done((f32[3,4,32,128]{3,2,1,0:T(8,128)S(1)}, f32[3,4,32,128]{3,2,1,0:T(8,128)S(1)}, u32[]{:S(2)}, u32[]{:S(2)}) %collective-permute-start.2) | collective-permute-done | bytes 196640 | tf_op jit(solution)/shard_map/ppermute | solution.py:24
  72.3 0.1 pad_maximum_fusion
  72.4 0.4 fusion.127
  72.8 0.2 fusion.128
  73.1 0.4 fusion.126
  73.5 2.1 %fusion.25 = f32[3,22,32,128]{3,2,1,0:T(8,128)S(1)} fusion(f32[3,4,32,128]{3,2,1,0:T(8,128)S(1)} %collective-permute-done.3, f32[3,16,32,128]{3,2,1,0:T(8,128)S(1)} %fusion.102, f32[3,4,32,128]{3,2,1,0:T(8,128)S(1)} %collective-permute-done.2, f32[3,24,32,128]{3,2,1,0:T(8,128)S(1)} %pad_maximum_fusion, f32[3,22,31,128]{3,2,1,0:T(8,128)S(1)} %get-tuple-element.23, ...), kind=kLoop, calls=%fused_computation.34 | loop fusion | flops 7569408 | bytes 12580864 | tf_op jit(solution)/shard_map/add | solution.py:101
  75.7 0.2 fusion.136
  75.9 0.3 fusion.134
  76.2 0.3 fusion.133
  76.6 1.3 %fusion.51 = f32[3,20,32,128]{3,2,1,0:T(8,128)S(1)} fusion(f32[3,22,32,128]{3,2,1,0:T(8,128)S(1)} %fusion.25, f32[3,20,1,128]{3,2,1,0:T(1,128)S(1)} %get-tuple-element.37, f32[3,20,31,128]{3,2,1,0:T(8,128)S(1)} %get-tuple-element.39, f32[3,20,31,128]{3,2,1,0:T(8,128)S(1)} %get-tuple-element.38, f32[3,20,1,128]{3,2,1,0:T(1,128)S(1)} %get-tuple-element.36, ...), kind=kLoop, calls=%fused_computation.74 | loop fusion | flops 5406720 | bytes 11141120 | tf_op jit(solution)/shard_map/add | solution.py:101
  77.9 0.2 fusion.146
  78.1 0.3 fusion.144
  78.4 0.3 fusion.143
  78.7 1.2 %fusion.73 = f32[3,18,32,128]{3,2,1,0:T(8,128)S(1)} fusion(f32[3,20,32,128]{3,2,1,0:T(8,128)S(1)} %fusion.51, f32[3,18,1,128]{3,2,1,0:T(1,128)S(1)} %get-tuple-element.59, f32[3,18,31,128]{3,2,1,0:T(8,128)S(1)} %get-tuple-element.61, f32[3,18,31,128]{3,2,1,0:T(8,128)S(1)} %get-tuple-element.60, f32[3,18,1,128]{3,2,1,0:T(1,128)S(1)} %get-tuple-element.58, ...), kind=kLoop, calls=%fused_computation.108 | loop fusion | flops 4866048 | bytes 10027008 | tf_op jit(solution)/shard_map/add | solution.py:101
  80.0 0.1 fusion.154
  80.2 0.3 fusion.152
  80.5 0.3 fusion.151
  80.8 1.1 %fusion.95 = f32[3,16,32,128]{3,2,1,0:T(8,128)S(1)} fusion(f32[3,16,32,128]{3,2,1,0:T(8,128)S(1)} %fusion.102, f32[3,18,32,128]{3,2,1,0:T(8,128)S(1)} %fusion.73, f32[3,16,1,128]{3,2,1,0:T(1,128)S(1)} %get-tuple-element.75, f32[3,16,31,128]{3,2,1,0:T(8,128)S(1)} %get-tuple-element.77, f32[3,16,31,128]{3,2,1,0:T(8,128)S(1)} %get-tuple-element.76, ...), kind=kLoop, calls=%fused_computation.142 | loop fusion | flops 4325376 | bytes 8912896 | tf_op jit(solution)/shard_map/add | solution.py:101
  81.9 0.1 collective-permute-start.8
  82.0 5.4 %collective-permute-start.9 = (f32[3,4,32,128]{3,2,1,0:T(8,128)S(1)}, f32[3,4,32,128]{3,2,1,0:T(8,128)S(1)}, u32[]{:S(2)}, u32[]{:S(2)}) collective-permute-start(f32[3,4,32,128]{3,2,1,0:T(8,128)S(1)} %get-tuple-element.79), channel_id=1, source_target_pairs={{1,0},{2,1},{3,2},{4,3},{5,4},{6,5},{7,6},{8,7},{9,8},{10,9},{11,1... | collective-permute-start | bytes 589832 | tf_op jit(solution)/shard_map/ppermute | solution.py:27
  87.4 2.7 %collective-permute-done.8 = f32[3,4,32,128]{3,2,1,0:T(8,128)S(1)} collective-permute-done((f32[3,4,32,128]{3,2,1,0:T(8,128)S(1)}, f32[3,4,32,128]{3,2,1,0:T(8,128)S(1)}, u32[]{:S(2)}, u32[]{:S(2)}) %collective-permute-start.8) | collective-permute-done | bytes 196640 | tf_op jit(solution)/shard_map/ppermute | solution.py:24
  90.1 0.1 pad_maximum_fusion.1
  90.2 0.4 fusion.124
  90.6 0.2 fusion.125
  90.9 0.4 fusion.123
  91.2 2.1 %fusion.10 = f32[3,22,32,128]{3,2,1,0:T(8,128)S(1)} fusion(f32[3,4,32,128]{3,2,1,0:T(8,128)S(1)} %collective-permute-done.9, f32[3,16,32,128]{3,2,1,0:T(8,128)S(1)} %fusion.95, f32[3,4,32,128]{3,2,1,0:T(8,128)S(1)} %collective-permute-done.8, f32[3,24,32,128]{3,2,1,0:T(8,128)S(1)} %pad_maximum_fusion.1, f32[3,22,31,128]{3,2,1,0:T(8,128)S(1)} %get-tuple-element.17, ...), kind=kLoop, calls=%fused_computation.13 | loop fusion | flops 7569408 | bytes 13367296 | tf_op jit(solution)/shard_map/add | solution.py:101
  93.4 0.2 fusion.132
  93.7 0.3 fusion.130
  94.0 0.3 fusion.129
  94.4 1.3 %fusion.40 = f32[3,20,32,128]{3,2,1,0:T(8,128)S(1)} fusion(f32[3,22,32,128]{3,2,1,0:T(8,128)S(1)} %fusion.10, f32[3,20,1,128]{3,2,1,0:T(1,128)S(1)} %get-tuple-element.29, f32[3,20,31,128]{3,2,1,0:T(8,128)S(1)} %get-tuple-element.31, f32[3,20,31,128]{3,2,1,0:T(8,128)S(1)} %get-tuple-element.30, f32[3,20,1,128]{3,2,1,0:T(1,128)S(1)} %get-tuple-element.28, ...), kind=kLoop, calls=%fused_computation.61 | loop fusion | flops 5406720 | bytes 11141120 | tf_op jit(solution)/shard_map/add | solution.py:101
  95.7 0.2 fusion.142
  95.9 0.3 fusion.140
  96.2 0.3 fusion.139
  96.5 1.2 %fusion.62 = f32[3,18,32,128]{3,2,1,0:T(8,128)S(1)} fusion(f32[3,20,32,128]{3,2,1,0:T(8,128)S(1)} %fusion.40, f32[3,18,1,128]{3,2,1,0:T(1,128)S(1)} %get-tuple-element.51, f32[3,18,31,128]{3,2,1,0:T(8,128)S(1)} %get-tuple-element.53, f32[3,18,31,128]{3,2,1,0:T(8,128)S(1)} %get-tuple-element.52, f32[3,18,1,128]{3,2,1,0:T(1,128)S(1)} %get-tuple-element.50, ...), kind=kLoop, calls=%fused_computation.95 | loop fusion | flops 4866048 | bytes 10027008 | tf_op jit(solution)/shard_map/add | solution.py:101
  97.8 0.1 fusion.147
  98.0 0.3 fusion.150
  98.3 0.3 fusion.149
  98.6 2.0 %fusion.105 = f32[1,3,16,32,128]{4,3,2,1,0:T(8,128)} fusion(f32[3,16,32,128]{3,2,1,0:T(8,128)S(1)} %fusion.102, f32[3,16,32,127]{3,2,1,0:T(8,128)S(1)} %get-tuple-element.67, f32[3,16,32,1]{3,2,1,0:T(8,128)S(1)} %get-tuple-element.69, f32[3,16,32,1]{3,2,1,0:T(8,128)S(1)} %get-tuple-element.68, f32[3,16,32,127]{3,2,1,0:T(8,128)S(1)} %get-tuple-element.66, ...), kind=kLoop, calls=%fused_computation.166 | loop fusion | flops 4325376 | bytes 8912896 | tf_op jit(solution)/shard_map/broadcast_in_dim | solution.py:151
  (63 shorter events, 1.4 us)
Async XLA Ops:
  0.0 1.4 %copy-start = (f32[1,3,16,32,128]{4,3,2,1,0:T(8,128)S(1)}, f32[1,3,16,32,128]{4,3,2,1,0:T(8,128)}, u32[]{:S(2)}) copy-start(f32[1,3,16,32,128]{4,3,2,1,0:T(8,128)} %param.2) | copy-start | bytes 2359300
  3.3 22.7 %all-to-all-start = ((f32[16,4,4096]{2,1,0:T(4,128)}), f32[16,4,4096]{2,1,0:T(4,128)S(1)}, u32[]{:S(2)}, u32[]{:S(2)}) async-start(f32[16,4,4096]{2,1,0:T(4,128)} %copy.4), calls=%async_computation | async-start | bytes 2097152 | tf_op jit(solution)/shard_map/all_to_all | solution.py:39
  10.8 45.8 %collective-permute-start = (f32[3,1,32,128]{3,2,1,0:T(8,128)}, f32[3,1,32,128]{3,2,1,0:T(8,128)S(1)}, u32[]{:S(2)}, u32[]{:S(2)}) collective-permute-start(f32[3,1,32,128]{3,2,1,0:T(8,128)} %get-tuple-element.92), channel_id=1, source_target_pairs={{1,0},{2,1},{3,2},{4,3},{5,4},{6,5},{7,6},{8,7},{9,8},{10,9},{11,1... | collective-permute-start | bytes 147464 | tf_op jit(solution)/shard_map/ppermute | solution.py:27
  18.7 37.9 %collective-permute-start.1 = (f32[3,1,32,128]{3,2,1,0:T(8,128)}, f32[3,1,32,128]{3,2,1,0:T(8,128)S(1)}, u32[]{:S(2)}, u32[]{:S(2)}) collective-permute-start(f32[3,1,32,128]{3,2,1,0:T(8,128)} %get-tuple-element.93), channel_id=1, source_target_pairs={{0,1},{1,2},{2,3},{3,4},{4,5},{5,6},{6,7},{7,8},{8,9},{9,10},{10,1... | collective-permute-start | bytes 147464 | tf_op jit(solution)/shard_map/ppermute | solution.py:24
  27.5 20.3 %all-to-all-start.1 = ((f32[16,4,4096]{2,1,0:T(4,128)}), f32[16,4,4096]{2,1,0:T(4,128)S(1)}, u32[]{:S(2)}, u32[]{:S(2)}) async-start(f32[16,4,4096]{2,1,0:T(4,128)} %broadcast_in_dim.4), calls=%async_computation.1 | async-start | bytes 2097152 | tf_op jit(solution)/shard_map/all_to_all | solution.py:45
  47.8 8.7 %copy-start.1 = (f32[3,16,32,127]{3,2,1,0:T(8,128)S(1)}, f32[3,16,32,127]{3,2,1,0:T(8,128)}, u32[]{:S(2)}) copy-start(f32[3,16,32,127]{3,2,1,0:T(8,128)} %get-tuple-element.86) | copy-start | bytes 2340868
  47.8 8.8 %copy-start.2 = (f32[3,16,32,127]{3,2,1,0:T(8,128)S(1)}, f32[3,16,32,127]{3,2,1,0:T(8,128)}, u32[]{:S(2)}) copy-start(f32[3,16,32,127]{3,2,1,0:T(8,128)} %get-tuple-element.87) | copy-start | bytes 2340868
  47.8 8.8 %copy-start.3 = (f32[3,16,31,128]{3,2,1,0:T(8,128)S(1)}, f32[3,16,31,128]{3,2,1,0:T(8,128)}, u32[]{:S(2)}) copy-start(f32[3,16,31,128]{3,2,1,0:T(8,128)} %get-tuple-element.90) | copy-start | bytes 2285572
  49.2 15.0 %collective-permute-start.7 = (f32[5,32,128]{2,1,0:T(8,128)S(1)}, f32[5,32,128]{2,1,0:T(8,128)S(1)}, u32[]{:S(2)}, u32[]{:S(2)}) collective-permute-start(f32[5,32,128]{2,1,0:T(8,128)S(1)} %bitcast.32), channel_id=1, source_target_pairs={{1,0},{2,1},{3,2},{4,3},{5,4},{6,5},{7,6},{8,7},{9,8},{10,9},{11,1... | collective-permute-start | bytes 245768 | tf_op jit(solution)/shard_map/ppermute | solution.py:27
  56.6 12.7 %collective-permute-start.6 = (f32[5,32,128]{2,1,0:T(8,128)S(1)}, f32[5,32,128]{2,1,0:T(8,128)S(1)}, u32[]{:S(2)}, u32[]{:S(2)}) collective-permute-start(f32[5,32,128]{2,1,0:T(8,128)S(1)} %bitcast.31), channel_id=1, source_target_pairs={{0,1},{1,2},{2,3},{3,4},{4,5},{5,6},{6,7},{7,8},{8,9},{9,10},{10,1... | collective-permute-start | bytes 245768 | tf_op jit(solution)/shard_map/ppermute | solution.py:24
  59.0 12.2 %collective-permute-start.4 = (f32[3,3,32,128]{3,2,1,0:T(8,128)S(1)}, f32[3,3,32,128]{3,2,1,0:T(8,128)S(1)}, u32[]{:S(2)}, u32[]{:S(2)}) collective-permute-start(f32[3,3,32,128]{3,2,1,0:T(8,128)S(1)} %get-tuple-element.80), channel_id=1, source_target_pairs={{0,1},{1,2},{2,3},{3,4},{4,5},{5,6},{6,7},{7,8},{8,9},{9,10},{10,1... | collective-permute-start | bytes 442376 | tf_op jit(solution)/shard_map/ppermute | solution.py:24
  59.1 12.1 %collective-permute-start.5 = (f32[3,3,32,128]{3,2,1,0:T(8,128)S(1)}, f32[3,3,32,128]{3,2,1,0:T(8,128)S(1)}, u32[]{:S(2)}, u32[]{:S(2)}) collective-permute-start(f32[3,3,32,128]{3,2,1,0:T(8,128)S(1)} %get-tuple-element.81), channel_id=1, source_target_pairs={{1,0},{2,1},{3,2},{4,3},{5,4},{6,5},{7,6},{8,7},{9,8},{10,9},{11,1... | collective-permute-start | bytes 442376 | tf_op jit(solution)/shard_map/ppermute | solution.py:27
  64.2 8.1 %collective-permute-start.2 = (f32[3,4,32,128]{3,2,1,0:T(8,128)S(1)}, f32[3,4,32,128]{3,2,1,0:T(8,128)S(1)}, u32[]{:S(2)}, u32[]{:S(2)}) collective-permute-start(f32[3,4,32,128]{3,2,1,0:T(8,128)S(1)} %get-tuple-element.82), channel_id=1, source_target_pairs={{0,1},{1,2},{2,3},{3,4},{4,5},{5,6},{6,7},{7,8},{8,9},{9,10},{10,1... | collective-permute-start | bytes 589832 | tf_op jit(solution)/shard_map/ppermute | solution.py:24
  64.2 8.1 %collective-permute-start.3 = (f32[3,4,32,128]{3,2,1,0:T(8,128)S(1)}, f32[3,4,32,128]{3,2,1,0:T(8,128)S(1)}, u32[]{:S(2)}, u32[]{:S(2)}) collective-permute-start(f32[3,4,32,128]{3,2,1,0:T(8,128)S(1)} %get-tuple-element.83), channel_id=1, source_target_pairs={{1,0},{2,1},{3,2},{4,3},{5,4},{6,5},{7,6},{8,7},{9,8},{10,9},{11,1... | collective-permute-start | bytes 589832 | tf_op jit(solution)/shard_map/ppermute | solution.py:27
  81.9 8.2 %collective-permute-start.8 = (f32[3,4,32,128]{3,2,1,0:T(8,128)S(1)}, f32[3,4,32,128]{3,2,1,0:T(8,128)S(1)}, u32[]{:S(2)}, u32[]{:S(2)}) collective-permute-start(f32[3,4,32,128]{3,2,1,0:T(8,128)S(1)} %get-tuple-element.78), channel_id=1, source_target_pairs={{0,1},{1,2},{2,3},{3,4},{4,5},{5,6},{6,7},{7,8},{8,9},{9,10},{10,1... | collective-permute-start | bytes 589832 | tf_op jit(solution)/shard_map/ppermute | solution.py:24
  82.0 8.1 %collective-permute-start.9 = (f32[3,4,32,128]{3,2,1,0:T(8,128)S(1)}, f32[3,4,32,128]{3,2,1,0:T(8,128)S(1)}, u32[]{:S(2)}, u32[]{:S(2)}) collective-permute-start(f32[3,4,32,128]{3,2,1,0:T(8,128)S(1)} %get-tuple-element.79), channel_id=1, source_target_pairs={{1,0},{2,1},{3,2},{4,3},{5,4},{6,5},{7,6},{8,7},{9,8},{10,9},{11,1... | collective-permute-start | bytes 589832 | tf_op jit(solution)/shard_map/ppermute | solution.py:27
where the time goes:
time: 102 us; the launch traced here: 101 us
  starting transfers between devices  42.6 us (42%)
  waiting for transfers between devices  23.7 us (23%)
  other arithmetic  18.3 us (18%)
  local copies, waits for them, and re-layouts  15.2 us (15%)
    ppermute x5, starting transfers between devices, with_halo(): lax.ppermute(lax.slice_in_dim(block, 0, width, axis=dim), axis, backward)  30.9 us
    all_to_all x1, waiting for transfers between devices, sent_to_all(): return lax.all_to_all(copies, axis, split_axis=0, concat_axis=0, tiled=True)  12.5 us
    add x7, other arithmetic, sweep(): return center + step_size * (local_source - image) / diagonal  10.4 us
    all_to_all x1, waiting for transfers between devices, summed_on_arrival(): lax.all_to_all(cut_along(array, dim, devices), axis, 0, 0, tiled=True)  7.32 us
    all_to_all x1, starting transfers between devices, summed_on_arrival(): lax.all_to_all(cut_along(array, dim, devices), axis, 0, 0, tiled=True)  6.82 us
    slice x14, local copies, waits for them, and re-layouts, sweep(): jnp.roll(center, 1, 3)  4.8 us
    all_to_all x1, starting transfers between devices, sent_to_all(): return lax.all_to_all(copies, axis, split_axis=0, concat_axis=0, tiled=True)  4.74 us
    ppermute x5, waiting for transfers between devices, with_halo(): lax.ppermute(lax.slice_in_dim(block, block.shape[dim] - width, None, axis...  3.85 us
  transfers between devices with their start and end apart: 12, of which 4 were waited for; matrix products, arithmetic and copies ran while one was open for 10% of the time, Pallas kernels for 0%

commit v1 on v0

v1 whole, which is shorter than its diff:
```python
import functools
import math

import jax
import jax.numpy as jnp
from jax import lax
from jax.experimental import pallas as pl
from jax.experimental.pallas import tpu as pltpu
from jax.sharding import PartitionSpec as P

MESH = pl.DeviceIdType.MESH
SWEEPS = 8
TIME_STEP = 0.25
EDDY_COEFF = 1.0
BASE_VISCOSITY = 1.0
LOWER_EDGE = 0.1
UPPER_EDGE = 1.9

LAYERS = 16
TILES = 4
ROWS = 8
LANES = 128
CHIPS = 8
HALO = 4
ORDER = ((2, 1), (1, 1), (3, 1), (2, 0), (1, 0), (3, 0), (0, 1))


def step_sizes(sweep_count):
    middle = (UPPER_EDGE + LOWER_EDGE) / 2
    radius = (UPPER_EDGE - LOWER_EDGE) / 2
    return [
        1.0 / (middle + radius * math.cos(math.pi * (2 * position + 1) / (2 * sweep_count)))
        for position in range(sweep_count)
    ]


def shifted_chip(chip, dx, dy):
    x, y = chip // 2, lax.rem(chip, 2)
    return lax.rem(x + dx, 4) * 2 + lax.rem(y + dy, 2)


def kernel(
    vel_ref, force_ref, out_ref,
    vel, force, partner_vel, sums, arrived, flow, nu, weights, source, field_a, field_b, field_c, halo_low, halo_high,
    load_sem, pair_sem, rs_send, rs_recv, ag_send, ag_recv, fw_send, fw_recv,
    vh_send, vh_recv, nu_send, nu_recv, src_send, src_recv, mid_send, mid_recv,
):
    member, sub = lax.axis_index("member"), lax.axis_index("sub")
    chip, core = member // 2, lax.rem(member, 2)
    subs = lax.axis_size("sub")
    above = (member, lax.rem(sub + 1, subs))
    below = (member, lax.rem(sub + subs - 1, subs))
    partner = (chip * 2 + 1 - core, sub)
    peers = [(shifted_chip(chip, dx, dy) * 2 + core, sub) for dx, dy in ORDER]
    targets = [shifted_chip(chip, dx, dy) for dx, dy in ORDER]
    origins = [shifted_chip(chip, 4 - dx, dy) for dx, dy in ORDER]

    def remote(src, dst, send, recv, device):
        return pltpu.make_async_remote_copy(
            src_ref=src, dst_ref=dst, send_sem=send, recv_sem=recv, device_id=device, device_id_type=MESH
        )

    load_vel = pltpu.make_async_copy(vel_ref, vel.at[:, pl.ds(1, LAYERS)], load_sem.at[0])
    load_force = pltpu.make_async_copy(force_ref, force, load_sem.at[1])
    load_vel.start()
    load_force.start()

    barrier = pltpu.get_barrier_semaphore()
    greeted = [*peers, partner, above, below]
    for device in greeted:
        pl.semaphore_signal(barrier, inc=1, device_id=device, device_id_type=MESH)
    pl.semaphore_wait(barrier, len(greeted))

    pair = remote(
        vel_ref.at[:, pl.ds((1 - core) * CHIPS, CHIPS)], partner_vel, pair_sem.at[0], pair_sem.at[1], partner
    )
    pair.start()
    load_vel.wait()
    pair.wait_recv()

    rs_copies = []
    for tile in range(TILES):
        rows = pl.ds(tile, ROWS, stride=TILES)

        def pair_sums(target, tile=tile, rows=rows):
            squares = None
            for axis in range(3):
                mine = vel[axis, 1 + core * CHIPS + target, rows, :]
                other = partner_vel[axis, target, rows, :]
                sums[tile, target, axis] = mine + other
                term = mine * mine + other * other
                squares = term if squares is None else squares + term
            sums[tile, target, 3] = squares

        for target in targets:
            pair_sums(target)
        pair_sums(chip)
        for place, target in enumerate(targets):
            copy = remote(
                sums.at[tile, target], arrived.at[tile, chip], rs_send.at[tile, place], rs_recv.at[tile, chip],
                peers[place],
            )
            copy.start()
            rs_copies.append(copy)

    vel_up = remote(vel_ref.at[:, LAYERS - 1], vel.at[:, 0], vh_send.at[0], vh_recv.at[0], above)
    vel_down = remote(vel_ref.at[:, 0], vel.at[:, LAYERS + 1], vh_send.at[1], vh_recv.at[1], below)
    vel_up.start()
    vel_down.start()

    own = core * CHIPS + chip
    ag_copies = []
    for tile in range(TILES):
        for origin in origins:
            remote(
                sums.at[tile, 0], arrived.at[tile, origin], rs_send.at[tile, 0], rs_recv.at[tile, origin], partner
            ).wait_recv()
        total = [
            (
                (sums[tile, chip, i] + arrived[tile, origins[0], i])
                + (arrived[tile, origins[1], i] + arrived[tile, origins[2], i])
            )
            + (
                (arrived[tile, origins[3], i] + arrived[tile, origins[4], i])
                + (arrived[tile, origins[5], i] + arrived[tile, origins[6], i])
            )
            for i in range(4)
        ]
        mean = [total[i] * (1.0 / 16) for i in range(3)]
        spread = total[3] * (1.0 / 16) - (mean[0] * mean[0] + mean[1] * mean[1] + mean[2] * mean[2])
        for i in range(3):
            flow[own, tile, i] = mean[i]
        flow[own, tile, 3] = BASE_VISCOSITY + EDDY_COEFF * TIME_STEP * spread
        for place in range(len(ORDER)):
            copy = remote(
                flow.at[own, tile], flow.at[own, tile], ag_send.at[tile, place], ag_recv.at[tile, chip], peers[place]
            )
            copy.start()
            ag_copies.append(copy)

    load_force.wait()
    vel_up.wait_recv()
    vel_down.wait_recv()

    def make_source(layer):
        for axis in range(3):
            tiles = [vel[axis, layer + 1, pl.ds(t, ROWS, stride=TILES), :] for t in range(TILES)]
            for t in range(TILES):
                rows = pl.ds(t, ROWS, stride=TILES)
                here = tiles[t]
                along_x = vel[axis, layer + 2, rows, :] - vel[axis, layer, rows, :]
                north = tiles[t + 1] if t + 1 < TILES else pltpu.roll(tiles[0], ROWS - 1, 0)
                south = tiles[t - 1] if t > 0 else pltpu.roll(tiles[TILES - 1], 1, 0)
                along_z = pltpu.roll(here, LANES - 1, 1) - pltpu.roll(here, 1, 1)
                moved = flow[layer, t, 0] * along_x + flow[layer, t, 1] * (north - south) + flow[layer, t, 2] * along_z
                field_a[axis, HALO + layer, t] = (
                    here + TIME_STEP * force[axis, layer, rows, :] - (0.5 * TIME_STEP) * moved
                )
        for t in range(TILES):
            nu[HALO + layer, t] = flow[layer, t, 3]

    def chip_at(k):
        return shifted_chip(chip, k // 2, lax.rem(k, 2))

    def forward(at):
        layer = core * CHIPS + at
        return remote(flow.at[layer], flow.at[layer], fw_send.at[at], fw_recv.at[at], partner)

    def gather_step(k, carry):
        @pl.when(k < CHIPS)
        def _():
            at = chip_at(k)
            layer = core * CHIPS + at

            @pl.when(k > 0)
            def _():
                for tile in range(TILES):
                    remote(
                        flow.at[layer, tile], flow.at[layer, tile], ag_send.at[tile, 0], ag_recv.at[tile, at], partner
                    ).wait_recv()

            forward(at).start()
            make_source(layer)

        @pl.when(k > 0)
        def _():
            at = chip_at(k - 1)
            layer = (1 - core) * CHIPS + at
            remote(flow.at[layer], flow.at[layer], fw_send.at[at], fw_recv.at[at], partner).wait_recv()
            make_source(layer)

        return carry

    lax.fori_loop(0, CHIPS + 1, gather_step, 0)

    low, high = pl.ds(HALO, HALO), pl.ds(LAYERS, HALO)
    before, after = pl.ds(0, HALO), pl.ds(HALO + LAYERS, HALO)
    nu_copies = [
        remote(nu.at[low], nu.at[after], nu_send.at[0], nu_recv.at[0], below),
        remote(nu.at[high], nu.at[before], nu_send.at[1], nu_recv.at[1], above),
    ]
    for copy in nu_copies:
        copy.start()

    def source_copies(axis):
        return [
            remote(
                field_a.at[axis, low], field_a.at[axis, after], src_send.at[0, axis], src_recv.at[0, axis], below
            ),
            remote(
                field_a.at[axis, high], field_a.at[axis, before], src_send.at[1, axis], src_recv.at[1, axis], above
            ),
        ]

    for axis in range(3):
        for copy in source_copies(axis):
            copy.start()

    def make_weights(layer):
        centre = [nu[layer, t] for t in range(TILES)]
        for t in range(TILES):
            here = centre[t]
            north = centre[t + 1] if t + 1 < TILES else pltpu.roll(centre[0], ROWS - 1, 0)
            south = centre[t - 1] if t > 0 else pltpu.roll(centre[TILES - 1], 1, 0)
            around = (
                nu[layer + 1, t], nu[layer - 1, t], north, south,
                pltpu.roll(here, LANES - 1, 1), pltpu.roll(here, 1, 1),
            )
            faces = [here + other for other in around]
            total = ((faces[0] + faces[1]) + (faces[2] + faces[3])) + (faces[4] + faces[5])
            inverse = 1.0 / (1.0 + (0.5 * TIME_STEP) * total)
            scaled = (0.5 * TIME_STEP) * inverse
            for i in range(6):
                weights[layer, i, t] = faces[i] * scaled
            weights[layer, 6, t] = inverse

    def scale_source(layer, axis):
        for t in range(TILES):
            source[axis, layer, t] = field_a[axis, layer, t] * weights[layer, 6, t]

    def inner_weights(layer, carry):
        make_weights(layer)
        for axis in range(3):
            scale_source(layer, axis)
        return carry

    lax.fori_loop(HALO + 1, HALO + LAYERS - 1, inner_weights, 0)

    sizes = step_sizes(SWEEPS)

    def field_at(level):
        if level % HALO == 0:
            return field_a
        return (field_c, field_b)[level % 2]

    def sweep_tile(level, layer, axis, t, tiles, factors):
        old, new = field_at(level - 1), field_at(level)
        here = tiles[t]
        north = tiles[t + 1] if t + 1 < TILES else pltpu.roll(tiles[0], ROWS - 1, 0)
        south = tiles[t - 1] if t > 0 else pltpu.roll(tiles[TILES - 1], 1, 0)
        part_x = factors[0] * old[axis, layer + 1, t] + factors[1] * old[axis, layer - 1, t]
        part_y = factors[2] * north + factors[3] * south
        part_z = factors[4] * pltpu.roll(here, LANES - 1, 1) + factors[5] * pltpu.roll(here, 1, 1)
        change = ((source[axis, layer, t] - here) + part_x) + (part_y + part_z)
        value = here + sizes[level - 1] * change
        if level == SWEEPS:
            out_ref[axis, layer - HALO, pl.ds(t, ROWS, stride=TILES), :] = value
        else:
            new[axis, layer, t] = value

    def sweep_layer(level, layer, axes):
        old = field_at(level - 1)
        tiles = [[old[axis, layer, t] for t in range(TILES)] for axis in axes]
        for t in range(TILES):
            factors = [weights[layer, i, t] for i in range(6)]
            for axis, row in zip(axes, tiles):
                sweep_tile(level, layer, axis, t, row, factors)

    def sweep_inner(level, margin):
        def body(layer, carry):
            sweep_layer(level, layer, range(3))
            return carry

        lax.fori_loop(HALO + margin, HALO + LAYERS - margin, body, 0)

    def sweep_outer(level, margin, axis):
        for layer in range(margin - HALO, margin):
            sweep_layer(level, HALO + layer, [axis])
            sweep_layer(level, HALO + LAYERS - 1 - layer, [axis])

    for level in range(1, HALO + 1):
        sweep_inner(level, level)
    for copy in nu_copies:
        copy.wait_recv()

    def outer_weights(layer, carry):
        make_weights(layer)
        make_weights(layer + LAYERS + HALO - 2)
        return carry

    lax.fori_loop(1, HALO + 1, outer_weights, 0)

    def field_copies(axis):
        return [
            remote(field_a.at[axis, low], halo_high.at[axis], mid_send.at[0, axis], mid_recv.at[0, axis], below),
            remote(field_a.at[axis, high], halo_low.at[axis], mid_send.at[1, axis], mid_recv.at[1, axis], above),
        ]

    def first_outer(axis, carry):
        for copy in source_copies(axis):
            copy.wait()
        for layer in range(1, HALO + 1):
            scale_source(layer, axis)
            scale_source(layer + LAYERS + HALO - 2, axis)
        for level in range(1, HALO + 1):
            sweep_outer(level, level, axis)
        for copy in field_copies(axis):
            copy.start()
        return carry

    lax.fori_loop(0, 3, first_outer, 0)
    for level in range(1, HALO + 1):
        sweep_inner(HALO + level, level)

    def second_outer(axis, carry):
        for copy in field_copies(axis):
            copy.wait_recv()
        for layer in range(HALO):
            for t in range(TILES):
                field_a[axis, layer, t] = halo_low[axis, layer, t]
                field_a[axis, HALO + LAYERS + layer, t] = halo_high[axis, layer, t]
        for level in range(1, HALO + 1):
            sweep_outer(HALO + level, level, axis)
        return carry

    lax.fori_loop(0, 3, second_outer, 0)

    for copy in (pair, vel_up, vel_down, *nu_copies, *rs_copies, *ag_copies):
        copy.wait_send()

    def finish(at, carry):
        forward(at).wait_send()
        return carry

    lax.fori_loop(0, CHIPS, finish, 0)

    def finish_field(axis, carry):
        for copy in field_copies(axis):
            copy.wait_send()
        return carry

    lax.fori_loop(0, 3, finish_field, 0)


def per_device(velocity, forcing):
    f32 = jnp.float32
    full = LAYERS + 2 * HALO
    dma = pltpu.SemaphoreType.DMA
    tile = (ROWS, LANES)
    plane = (TILES * ROWS, LANES)
    result = pl.pallas_call(
        kernel,
        out_shape=jax.ShapeDtypeStruct(velocity.shape[1:], f32),
        in_specs=[pl.BlockSpec(memory_space=pltpu.MemorySpace.HBM)] * 2,
        out_specs=pl.BlockSpec(memory_space=pltpu.VMEM),
        scratch_shapes=[
            pltpu.VMEM((3, LAYERS + 2, *plane), f32),
            pltpu.VMEM((3, LAYERS, *plane), f32),
            pltpu.VMEM((3, CHIPS, *plane), f32),
            pltpu.VMEM((TILES, CHIPS, 4, *tile), f32),
            pltpu.VMEM((TILES, CHIPS, 4, *tile), f32),
            pltpu.VMEM((LAYERS, TILES, 4, *tile), f32),
            pltpu.VMEM((full, TILES, *tile), f32),
            pltpu.VMEM((full, 7, TILES, *tile), f32),
            pltpu.VMEM((3, full, TILES, *tile), f32),
            pltpu.VMEM((3, full, TILES, *tile), f32),
            pltpu.VMEM((3, full, TILES, *tile), f32),
            pltpu.VMEM((3, full, TILES, *tile), f32),
            pltpu.VMEM((3, HALO, TILES, *tile), f32),
            pltpu.VMEM((3, HALO, TILES, *tile), f32),
            dma((2,)), dma((2,)),
            dma((TILES, CHIPS)), dma((TILES, CHIPS)),
            dma((TILES, CHIPS)), dma((TILES, CHIPS)),
            dma((CHIPS,)), dma((CHIPS,)),
            dma((2,)), dma((2,)),
            dma((2,)), dma((2,)),
            dma((2, 3)), dma((2, 3)),
            dma((2, 3)), dma((2, 3)),
        ],
        compiler_params=pltpu.CompilerParams(
            collective_id=0, has_side_effects=True, vmem_limit_bytes=40 * 1024 * 1024
        ),
    )(
        pltpu.with_memory_space_constraint(velocity[0], pltpu.MemorySpace.HBM),
        pltpu.with_memory_space_constraint(forcing[0], pltpu.MemorySpace.HBM),
    )
    return result[None]


def solution(mesh):
    spec = P("member", None, "sub", None, None)
    return jax.shard_map(per_device, mesh=mesh, in_specs=(spec, spec), out_specs=spec, check_vma=False)
```

time: 102 us -> 48.1 us (0.47); the launches traced: 101 us -> 48 us
  Pallas kernels: 0 us -> 47.2 us
  starting transfers between devices: 42.6 us -> 0 us
  waiting for transfers between devices: 23.7 us -> 0 us
  other arithmetic: 18.3 us -> 0 us
  local copies, waits for them, and re-layouts: 15.2 us -> 0.88 us
    pallas_call x0 -> x1, Pallas kernels: none -> 47.2 us  [per_device(): pl.pallas_call(kernel, out_shape=jax.ShapeDtypeStruct(velocity.shape[1:],...]
    ppermute x10 -> x0, starting transfers between devices: 31.1 us -> none  [the longest x5 30.9 us: with_halo(): lax.ppermute(lax.slice_in_dim(block, 0, width, axis=dim), axis, backward)]
    all_to_all x2 -> x0, waiting for transfers between devices: 19.9 us -> none  [the longest x1 12.5 us: sent_to_all(): return lax.all_to_all(copies, axis, split_axis=0, concat_axis=0, tiled=True)]
    add x10 -> x0, other arithmetic: 13.3 us -> none  [the longest x7 10.4 us: sweep(): return center + step_size * (local_source - image) / diagonal]
    slice x70 -> x0, local copies, waits for them, and re-layouts: 12.1 us -> none  [the longest x14 4.8 us: sweep(): jnp.roll(center, 1, 3)]
    all_to_all x2 -> x0, starting transfers between devices: 11.6 us -> none  [the longest x1 6.82 us: summed_on_arrival(): lax.all_to_all(cut_along(array, dim, devices), axis, 0, 0, tiled=True)]
    ppermute x10 -> x0, waiting for transfers between devices: 3.87 us -> none  [the longest x5 3.85 us: with_halo(): lax.ppermute(lax.slice_in_dim(block, block.shape[dim] - width, None, axis...]
    broadcast_in_dim x1 -> x0, other arithmetic: 1.95 us -> none  [per_device(): return field[None]]
  transfers between devices with their start and end apart: 12 -> 0, of which waited for: 4 -> 0; matrix products, arithmetic and copies ran while one was open for 10% -> 0% of each run, Pallas kernels for 0% -> 0%
where the time goes in v1:
time: 48.1 us; the launch traced here: 48 us
  Pallas kernels  47.2 us (98%)
  local copies, waits for them, and re-layouts  0.88 us (2%)
    pallas_call x1, Pallas kernels, per_device(): pl.pallas_call(kernel, out_shape=jax.ShapeDtypeStruct(velocity.shape[1:],...  47.2 us

profile of v1, /device:TPU:1, one launch (start us, length us, event | category | flops | bytes accessed | tf_op | source)
XLA Modules:
  0.0 48.0 jit_solution(17762109846968398629)
XLA Ops:
  0.0 47.2 %shard_map.28 = f32[3,16,32,128]{3,2,1,0:T(8,128)S(1)} custom-call(f32[3,16,32,128]{3,2,1,0:T(8,128)} %bitcast.4, f32[3,16,32,128]{3,2,1,0:T(8,128)} %bitcast.5), custom_call_target="tpu_custom_call" | custom-call | tf_op jit(solution)/shard_map/pallas_call | solution.py:361
  47.2 0.9 %copy.4 = f32[1,3,16,32,128]{4,3,2,1,0:T(8,128)} copy(f32[1,3,16,32,128]{4,3,2,1,0:T(8,128)S(1)} %bitcast.3) | data formatting | bytes 1572864

commit v2 on v1

--- a/solution.py
+++ b/solution.py
@@ -22,6 +22,8 @@
 LANES = 128
 CHIPS = 8
 HALO = 4
+PARTS = 4
+SPAN = TILES // PARTS
 ORDER = ((2, 1), (1, 1), (3, 1), (2, 0), (1, 0), (3, 0), (0, 1))
 
 
@@ -41,7 +43,7 @@
 
 def kernel(
     vel_ref, force_ref, out_ref,
-    vel, force, partner_vel, sums, arrived, flow, nu, weights, source, field_a, field_b, field_c, halo_low, halo_high,
+    vel, force, partner_vel, sums, arrived, flow, pre, slopes, nu, weights, source, field_a, field_b, field_c, halo_low, halo_high,
     load_sem, pair_sem, rs_send, rs_recv, ag_send, ag_recv, fw_send, fw_recv,
     vh_send, vh_recv, nu_send, nu_recv, src_send, src_recv, mid_send, mid_recv,
 ):
@@ -78,120 +80,120 @@
     load_vel.wait()
     pair.wait_recv()
 
-    rs_copies = []
-    for tile in range(TILES):
-        rows = pl.ds(tile, ROWS, stride=TILES)
-
-        def pair_sums(target, tile=tile, rows=rows):
+    vel_up = remote(vel_ref.at[:, LAYERS - 1], vel.at[:, 0], vh_send.at[0], vh_recv.at[0], above)
+    vel_down = remote(vel_ref.at[:, 0], vel.at[:, LAYERS + 1], vh_send.at[1], vh_recv.at[1], below)
+
+    def tile_rows(t):
+        return pl.ds(t, ROWS, stride=TILES)
+
+    def pair_sums(part, target):
+        for k in range(SPAN):
+            rows = tile_rows(part * SPAN + k)
             squares = None
             for axis in range(3):
                 mine = vel[axis, 1 + core * CHIPS + target, rows, :]
                 other = partner_vel[axis, target, rows, :]
-                sums[tile, target, axis] = mine + other
+                sums[part, target, k, axis] = mine + other
                 term = mine * mine + other * other
                 squares = term if squares is None else squares + term
-            sums[tile, target, 3] = squares
-
+            sums[part, target, k, 3] = squares
+
+    for part in range(PARTS):
         for target in targets:
-            pair_sums(target)
-        pair_sums(chip)
+            pair_sums(part, target)
+        pair_sums(part, chip)
         for place, target in enumerate(targets):
-            copy = remote(
-                sums.at[tile, target], arrived.at[tile, chip], rs_send.at[tile, place], rs_recv.at[tile, chip],
-                peers[place],
-            )
-            copy.start()
-            rs_copies.append(copy)
-
-    vel_up = remote(vel_ref.at[:, LAYERS - 1], vel.at[:, 0], vh_send.at[0], vh_recv.at[0], above)
-    vel_down = remote(vel_ref.at[:, 0], vel.at[:, LAYERS + 1], vh_send.at[1], vh_recv.at[1], below)
+            remote(
+                sums.at[part, target], arrived.at[part, chip], rs_send.at[0], rs_recv.at[part], peers[place]
+            ).start()
     vel_up.start()
     vel_down.start()
 
+    others = pl.ds(0, CHIPS - 1)
     own = core * CHIPS + chip
-    ag_copies = []
-    for tile in range(TILES):
-        for origin in origins:
-            remote(
-                sums.at[tile, 0], arrived.at[tile, origin], rs_send.at[tile, 0], rs_recv.at[tile, origin], partner
-            ).wait_recv()
-        total = [
-            (
-                (sums[tile, chip, i] + arrived[tile, origins[0], i])
-                + (arrived[tile, origins[1], i] + arrived[tile, origins[2], i])
-            )
-            + (
-                (arrived[tile, origins[3], i] + arrived[tile, origins[4], i])
-                + (arrived[tile, origins[5], i] + arrived[tile, origins[6], i])
-            )
-            for i in range(4)
-        ]
-        mean = [total[i] * (1.0 / 16) for i in range(3)]
-        spread = total[3] * (1.0 / 16) - (mean[0] * mean[0] + mean[1] * mean[1] + mean[2] * mean[2])
-        for i in range(3):
-            flow[own, tile, i] = mean[i]
-        flow[own, tile, 3] = BASE_VISCOSITY + EDDY_COEFF * TIME_STEP * spread
-        for place in range(len(ORDER)):
-            copy = remote(
-                flow.at[own, tile], flow.at[own, tile], ag_send.at[tile, place], ag_recv.at[tile, chip], peers[place]
-            )
-            copy.start()
-            ag_copies.append(copy)
+    for part in range(PARTS):
+        remote(
+            sums.at[part, others], arrived.at[part, others], rs_send.at[0], rs_recv.at[part], partner
+        ).wait_recv()
+        for k in range(SPAN):
+            tile = part * SPAN + k
+            total = [
+                (
+                    (sums[part, chip, k, i] + arrived[part, origins[0], k, i])
+                    + (arrived[part, origins[1], k, i] + arrived[part, origins[2], k, i])
+                )
+                + (
+                    (arrived[part, origins[3], k, i] + arrived[part, origins[4], k, i])
+                    + (arrived[part, origins[5], k, i] + arrived[part, origins[6], k, i])
+                )
+                for i in range(4)
+            ]
+            mean = [total[i] * (1.0 / 16) for i in range(3)]
+            spread = total[3] * (1.0 / 16) - (mean[0] * mean[0] + mean[1] * mean[1] + mean[2] * mean[2])
+            for i in range(3):
+                flow[own, tile, i] = mean[i]
+            flow[own, tile, 3] = BASE_VISCOSITY + EDDY_COEFF * TIME_STEP * spread
+        piece = flow.at[own, pl.ds(part * SPAN, SPAN)]
+        for peer in peers:
+            remote(piece, piece, ag_send.at[0], ag_recv.at[chip], peer).start()
 
     load_force.wait()
     vel_up.wait_recv()
     vel_down.wait_recv()
 
-    def make_source(layer):
+    def prepare(layer, carry):
         for axis in range(3):
-            tiles = [vel[axis, layer + 1, pl.ds(t, ROWS, stride=TILES), :] for t in range(TILES)]
+            tiles = [vel[axis, layer + 1, tile_rows(t), :] for t in range(TILES)]
             for t in range(TILES):
-                rows = pl.ds(t, ROWS, stride=TILES)
                 here = tiles[t]
-                along_x = vel[axis, layer + 2, rows, :] - vel[axis, layer, rows, :]
                 north = tiles[t + 1] if t + 1 < TILES else pltpu.roll(tiles[0], ROWS - 1, 0)
                 south = tiles[t - 1] if t > 0 else pltpu.roll(tiles[TILES - 1], 1, 0)
-                along_z = pltpu.roll(here, LANES - 1, 1) - pltpu.roll(here, 1, 1)
-                moved = flow[layer, t, 0] * along_x + flow[layer, t, 1] * (north - south) + flow[layer, t, 2] * along_z
-                field_a[axis, HALO + layer, t] = (
-                    here + TIME_STEP * force[axis, layer, rows, :] - (0.5 * TIME_STEP) * moved
+                gaps = (
+                    vel[axis, layer, tile_rows(t), :] - vel[axis, layer + 2, tile_rows(t), :],
+                    south - north,
+                    pltpu.roll(here, 1, 1) - pltpu.roll(here, LANES - 1, 1),
                 )
+                for i in range(3):
+                    slopes[layer, axis, i, t] = (0.5 * TIME_STEP) * gaps[i]
+                pre[layer, axis, t] = here + TIME_STEP * force[axis, layer, tile_rows(t), :]
+        return carry
+
+    lax.fori_loop(0, LAYERS, prepare, 0)
+
+    def make_source(layer):
         for t in range(TILES):
+            mean = [flow[layer, t, i] for i in range(3)]
             nu[HALO + layer, t] = flow[layer, t, 3]
+            for axis in range(3):
+                moved = mean[0] * slopes[layer, axis, 0, t] + mean[1] * slopes[layer, axis, 1, t]
+                field_a[axis, HALO + layer, t] = pre[layer, axis, t] + (moved + mean[2] * slopes[layer, axis, 2, t])
 
     def chip_at(k):
         return shifted_chip(chip, k // 2, lax.rem(k, 2))
 
     def forward(at):
         layer = core * CHIPS + at
-        return remote(flow.at[layer], flow.at[layer], fw_send.at[at], fw_recv.at[at], partner)
+        return remote(flow.at[layer], flow.at[layer], fw_send.at[0], fw_recv.at[at], partner)
+
+    forward(chip).start()
+    make_source(own)
 
     def gather_step(k, carry):
         @pl.when(k < CHIPS)
         def _():
             at = chip_at(k)
             layer = core * CHIPS + at
-
-            @pl.when(k > 0)
-            def _():
-                for tile in range(TILES):
-                    remote(
-                        flow.at[layer, tile], flow.at[layer, tile], ag_send.at[tile, 0], ag_recv.at[tile, at], partner
-                    ).wait_recv()
-
+            remote(flow.at[layer], flow.at[layer], ag_send.at[0], ag_recv.at[at], partner).wait_recv()
             forward(at).start()
             make_source(layer)
 
-        @pl.when(k > 0)
-        def _():
-            at = chip_at(k - 1)
-            layer = (1 - core) * CHIPS + at
-            remote(flow.at[layer], flow.at[layer], fw_send.at[at], fw_recv.at[at], partner).wait_recv()
-            make_source(layer)
-
-        return carry
-
-    lax.fori_loop(0, CHIPS + 1, gather_step, 0)
+        at = chip_at(k - 1)
+        layer = (1 - core) * CHIPS + at
+        remote(flow.at[layer], flow.at[layer], fw_send.at[0], fw_recv.at[at], partner).wait_recv()
+        make_source(layer)
+        return carry
+
+    lax.fori_loop(1, CHIPS + 1, gather_step, 0)
 
     low, high = pl.ds(HALO, HALO), pl.ds(LAYERS, HALO)
     before, after = pl.ds(0, HALO), pl.ds(HALO + LAYERS, HALO)
@@ -277,11 +279,12 @@
                 sweep_tile(level, layer, axis, t, row, factors)
 
     def sweep_inner(level, margin):
-        def body(layer, carry):
-            sweep_layer(level, layer, range(3))
+        def body(i, carry):
+            for k in range(2):
+                sweep_layer(level, HALO + margin + 2 * i + k, range(3))
             return carry
 
-        lax.fori_loop(HALO + margin, HALO + LAYERS - margin, body, 0)
+        lax.fori_loop(0, LAYERS // 2 - margin, body, 0)
 
     def sweep_outer(level, margin, axis):
         for layer in range(margin - HALO, margin):
@@ -290,8 +293,14 @@
 
     for level in range(1, HALO + 1):
         sweep_inner(level, level)
+    for copy in (pair, vel_up, vel_down):
+        copy.wait_send()
+    remote(sums.at[:, others], arrived.at[:, others], rs_send.at[0], rs_recv.at[0], partner).wait_send()
+    remote(sums.at[:, others], arrived.at[:, others], ag_send.at[0], ag_recv.at[0], partner).wait_send()
+    half = pl.ds(0, CHIPS)
+    remote(flow.at[half], flow.at[half], fw_send.at[0], fw_recv.at[0], partner).wait_send()
     for copy in nu_copies:
-        copy.wait_recv()
+        copy.wait()
 
     def outer_weights(layer, carry):
         make_weights(layer)
@@ -334,15 +343,6 @@
         return carry
 
     lax.fori_loop(0, 3, second_outer, 0)
-
-    for copy in (pair, vel_up, vel_down, *nu_copies, *rs_copies, *ag_copies):
-        copy.wait_send()
-
-    def finish(at, carry):
-        forward(at).wait_send()
-        return carry
-
-    lax.fori_loop(0, CHIPS, finish, 0)
 
     def finish_field(axis, carry):
         for copy in field_copies(axis):
@@ -367,9 +367,11 @@
             pltpu.VMEM((3, LAYERS + 2, *plane), f32),
             pltpu.VMEM((3, LAYERS, *plane), f32),
             pltpu.VMEM((3, CHIPS, *plane), f32),
-            pltpu.VMEM((TILES, CHIPS, 4, *tile), f32),
-            pltpu.VMEM((TILES, CHIPS, 4, *tile), f32),
+            pltpu.VMEM((PARTS, CHIPS, SPAN, 4, *tile), f32),
+            pltpu.VMEM((PARTS, CHIPS, SPAN, 4, *tile), f32),
             pltpu.VMEM((LAYERS, TILES, 4, *tile), f32),
+            pltpu.VMEM((LAYERS, 3, TILES, *tile), f32),
+            pltpu.VMEM((LAYERS, 3, 3, TILES, *tile), f32),
             pltpu.VMEM((full, TILES, *tile), f32),
             pltpu.VMEM((full, 7, TILES, *tile), f32),
             pltpu.VMEM((3, full, TILES, *tile), f32),
@@ -379,9 +381,9 @@
             pltpu.VMEM((3, HALO, TILES, *tile), f32),
             pltpu.VMEM((3, HALO, TILES, *tile), f32),
             dma((2,)), dma((2,)),
-            dma((TILES, CHIPS)), dma((TILES, CHIPS)),
-            dma((TILES, CHIPS)), dma((TILES, CHIPS)),
-            dma((CHIPS,)), dma((CHIPS,)),
+            dma((1,)), dma((PARTS,)),
+            dma((1,)), dma((CHIPS,)),
+            dma((1,)), dma((CHIPS,)),
             dma((2,)), dma((2,)),
             dma((2,)), dma((2,)),
             dma((2, 3)), dma((2, 3)),

time: 48.1 us -> 45.2 us (0.940)
  Pallas kernels: 47.2 us -> 44 us
    pallas_call x1, Pallas kernels: 47.2 us -> 44 us  [per_device(): pl.pallas_call(kernel, out_shape=jax.ShapeDtypeStruct(velocity.shape[1:],...]
where the time goes in v2:
time: 45.2 us; the launch traced here: 44.9 us
  Pallas kernels  44 us (97%)
  local copies, waits for them, and re-layouts  0.88 us (2%)
    pallas_call x1, Pallas kernels, per_device(): pl.pallas_call(kernel, out_shape=jax.ShapeDtypeStruct(velocity.shape[1:],...  44 us

profile of v2, /device:TPU:1, one launch (start us, length us, event | category | flops | bytes accessed | tf_op | source)
XLA Modules:
  0.0 44.9 jit_solution(6055066773559929405)
XLA Ops:
  0.0 44.0 %shard_map.28 = f32[3,16,32,128]{3,2,1,0:T(8,128)S(1)} custom-call(f32[3,16,32,128]{3,2,1,0:T(8,128)} %bitcast.4, f32[3,16,32,128]{3,2,1,0:T(8,128)} %bitcast.5), custom_call_target="tpu_custom_call" | custom-call | tf_op jit(solution)/shard_map/pallas_call | solution.py:361
  44.0 0.9 %copy.4 = f32[1,3,16,32,128]{4,3,2,1,0:T(8,128)} copy(f32[1,3,16,32,128]{4,3,2,1,0:T(8,128)S(1)} %bitcast.3) | data formatting | bytes 1572864

commit v3 on v2

--- a/solution.py
+++ b/solution.py
@@ -23,7 +23,6 @@
 CHIPS = 8
 HALO = 4
 PARTS = 4
-SPAN = TILES // PARTS
 ORDER = ((2, 1), (1, 1), (3, 1), (2, 0), (1, 0), (3, 0), (0, 1))
 
 
@@ -73,12 +72,18 @@
         pl.semaphore_signal(barrier, inc=1, device_id=device, device_id_type=MESH)
     pl.semaphore_wait(barrier, len(greeted))
 
-    pair = remote(
-        vel_ref.at[:, pl.ds((1 - core) * CHIPS, CHIPS)], partner_vel, pair_sem.at[0], pair_sem.at[1], partner
-    )
-    pair.start()
-    load_vel.wait()
-    pair.wait_recv()
+    def part_rows(part):
+        return pl.ds(part * ROWS, ROWS)
+
+    pairs = [
+        remote(
+            vel_ref.at[:, pl.ds((1 - core) * CHIPS, CHIPS), part_rows(part)], partner_vel.at[:, :, part_rows(part)],
+            pair_sem.at[0, part], pair_sem.at[1, part], partner,
+        )
+        for part in range(PARTS)
+    ]
+    for copy in pairs:
+        copy.start()
 
     vel_up = remote(vel_ref.at[:, LAYERS - 1], vel.at[:, 0], vh_send.at[0], vh_recv.at[0], above)
     vel_down = remote(vel_ref.at[:, 0], vel.at[:, LAYERS + 1], vh_send.at[1], vh_recv.at[1], below)
@@ -87,18 +92,18 @@
         return pl.ds(t, ROWS, stride=TILES)
 
     def pair_sums(part, target):
-        for k in range(SPAN):
-            rows = tile_rows(part * SPAN + k)
-            squares = None
-            for axis in range(3):
-                mine = vel[axis, 1 + core * CHIPS + target, rows, :]
-                other = partner_vel[axis, target, rows, :]
-                sums[part, target, k, axis] = mine + other
-                term = mine * mine + other * other
-                squares = term if squares is None else squares + term
-            sums[part, target, k, 3] = squares
-
+        squares = None
+        for axis in range(3):
+            mine = vel[axis, 1 + core * CHIPS + target, part_rows(part), :]
+            other = partner_vel[axis, target, part_rows(part), :]
+            sums[part, target, axis] = mine + other
+            term = mine * mine + other * other
+            squares = term if squares is None else squares + term
+        sums[part, target, 3] = squares
+
+    load_vel.wait()
     for part in range(PARTS):
+        pairs[part].wait_recv()
         for target in targets:
             pair_sums(part, target)
         pair_sums(part, chip)
@@ -115,25 +120,23 @@
         remote(
             sums.at[part, others], arrived.at[part, others], rs_send.at[0], rs_recv.at[part], partner
         ).wait_recv()
-        for k in range(SPAN):
-            tile = part * SPAN + k
-            total = [
-                (
-                    (sums[part, chip, k, i] + arrived[part, origins[0], k, i])
-                    + (arrived[part, origins[1], k, i] + arrived[part, origins[2], k, i])
-                )
-                + (
-                    (arrived[part, origins[3], k, i] + arrived[part, origins[4], k, i])
-                    + (arrived[part, origins[5], k, i] + arrived[part, origins[6], k, i])
-                )
-                for i in range(4)
-            ]
-            mean = [total[i] * (1.0 / 16) for i in range(3)]
-            spread = total[3] * (1.0 / 16) - (mean[0] * mean[0] + mean[1] * mean[1] + mean[2] * mean[2])
-            for i in range(3):
-                flow[own, tile, i] = mean[i]
-            flow[own, tile, 3] = BASE_VISCOSITY + EDDY_COEFF * TIME_STEP * spread
-        piece = flow.at[own, pl.ds(part * SPAN, SPAN)]
+        total = [
+            (
+                (sums[part, chip, i] + arrived[part, origins[0], i])
+                + (arrived[part, origins[1], i] + arrived[part, origins[2], i])
+            )
+            + (
+                (arrived[part, origins[3], i] + arrived[part, origins[4], i])
+                + (arrived[part, origins[5], i] + arrived[part, origins[6], i])
+            )
+            for i in range(4)
+        ]
+        mean = [total[i] * (1.0 / 16) for i in range(3)]
+        spread = total[3] * (1.0 / 16) - (mean[0] * mean[0] + mean[1] * mean[1] + mean[2] * mean[2])
+        for i in range(3):
+            flow[own, i, part_rows(part), :] = mean[i]
+        flow[own, 3, part_rows(part), :] = BASE_VISCOSITY + EDDY_COEFF * TIME_STEP * spread
+        piece = flow.at[own, :, part_rows(part)]
         for peer in peers:
             remote(piece, piece, ag_send.at[0], ag_recv.at[chip], peer).start()
 
@@ -162,8 +165,8 @@
 
     def make_source(layer):
         for t in range(TILES):
-            mean = [flow[layer, t, i] for i in range(3)]
-            nu[HALO + layer, t] = flow[layer, t, 3]
+            mean = [flow[layer, i, tile_rows(t), :] for i in range(3)]
+            nu[HALO + layer, t] = flow[layer, 3, tile_rows(t), :]
             for axis in range(3):
                 moved = mean[0] * slopes[layer, axis, 0, t] + mean[1] * slopes[layer, axis, 1, t]
                 field_a[axis, HALO + layer, t] = pre[layer, axis, t] + (moved + mean[2] * slopes[layer, axis, 2, t])
@@ -176,47 +179,64 @@
         return remote(flow.at[layer], flow.at[layer], fw_send.at[0], fw_recv.at[at], partner)
 
     forward(chip).start()
-    make_source(own)
 
     def gather_step(k, carry):
-        @pl.when(k < CHIPS)
-        def _():
-            at = chip_at(k)
-            layer = core * CHIPS + at
-            remote(flow.at[layer], flow.at[layer], ag_send.at[0], ag_recv.at[at], partner).wait_recv()
-            forward(at).start()
-            make_source(layer)
-
-        at = chip_at(k - 1)
-        layer = (1 - core) * CHIPS + at
-        remote(flow.at[layer], flow.at[layer], fw_send.at[0], fw_recv.at[at], partner).wait_recv()
-        make_source(layer)
-        return carry
-
-    lax.fori_loop(1, CHIPS + 1, gather_step, 0)
+        at = chip_at(k)
+        layer = core * CHIPS + at
+        remote(flow.at[layer], flow.at[layer], ag_send.at[0], ag_recv.at[at], partner).wait_recv()
+        forward(at).start()
+        return carry
+
+    lax.fori_loop(1, CHIPS, gather_step, 0)
+
+    def direct_sources(first):
+        def body(i, carry):
+            make_source(first + i)
+            return carry
+
+        lax.fori_loop(0, HALO, body, 0)
+
+    def forwarded_sources(first):
+        def body(i, carry):
+            at = first + i - (1 - core) * CHIPS
+            forward(at).wait_recv()
+            make_source(first + i)
+            return carry
+
+        lax.fori_loop(0, HALO, body, 0)
 
     low, high = pl.ds(HALO, HALO), pl.ds(LAYERS, HALO)
-    before, after = pl.ds(0, HALO), pl.ds(HALO + LAYERS, HALO)
-    nu_copies = [
-        remote(nu.at[low], nu.at[after], nu_send.at[0], nu_recv.at[0], below),
-        remote(nu.at[high], nu.at[before], nu_send.at[1], nu_recv.at[1], above),
-    ]
-    for copy in nu_copies:
-        copy.start()
-
-    def source_copies(axis):
-        return [
-            remote(
-                field_a.at[axis, low], field_a.at[axis, after], src_send.at[0, axis], src_recv.at[0, axis], below
-            ),
-            remote(
-                field_a.at[axis, high], field_a.at[axis, before], src_send.at[1, axis], src_recv.at[1, axis], above
-            ),
-        ]
-
-    for axis in range(3):
-        for copy in source_copies(axis):
-            copy.start()
+
+    def side_of(side):
+        device = (member, jnp.where(side == 1, above[1], below[1]))
+        return (
+            pl.ds(jnp.where(side == 1, LAYERS, HALO), HALO),
+            pl.ds(jnp.where(side == 1, 0, HALO + LAYERS), HALO),
+            device,
+        )
+
+    def nu_copy(side):
+        inside, outside, device = side_of(side)
+        return remote(nu.at[inside], nu.at[outside], nu_send.at[side], nu_recv.at[side], device)
+
+    def source_copy(side, axis):
+        inside, outside, device = side_of(side)
+        return remote(
+            field_a.at[axis, inside], field_a.at[axis, outside], src_send.at[side, axis], src_recv.at[side, axis],
+            device,
+        )
+
+    def send_side(side):
+        nu_copy(side).start()
+        for axis in range(3):
+            source_copy(side, axis).start()
+
+    direct_sources(core * (LAYERS - HALO))
+    send_side(core)
+    forwarded_sources((1 - core) * (LAYERS - HALO))
+    send_side(1 - core)
+    direct_sources(HALO + core * HALO)
+    forwarded_sources(HALO + (1 - core) * HALO)
 
     def make_weights(layer):
         centre = [nu[layer, t] for t in range(TILES)]
@@ -293,14 +313,14 @@
 
     for level in range(1, HALO + 1):
         sweep_inner(level, level)
-    for copy in (pair, vel_up, vel_down):
+    for copy in (*pairs, vel_up, vel_down):
         copy.wait_send()
     remote(sums.at[:, others], arrived.at[:, others], rs_send.at[0], rs_recv.at[0], partner).wait_send()
     remote(sums.at[:, others], arrived.at[:, others], ag_send.at[0], ag_recv.at[0], partner).wait_send()
     half = pl.ds(0, CHIPS)
     remote(flow.at[half], flow.at[half], fw_send.at[0], fw_recv.at[0], partner).wait_send()
-    for copy in nu_copies:
-        copy.wait()
+    for side in range(2):
+        nu_copy(side).wait()
 
     def outer_weights(layer, carry):
         make_weights(layer)
@@ -316,8 +336,8 @@
         ]
 
     def first_outer(axis, carry):
-        for copy in source_copies(axis):
-            copy.wait()
+        for side in range(2):
+            source_copy(side, axis).wait()
         for layer in range(1, HALO + 1):
             scale_source(layer, axis)
             scale_source(layer + LAYERS + HALO - 2, axis)
@@ -367,9 +387,9 @@
             pltpu.VMEM((3, LAYERS + 2, *plane), f32),
             pltpu.VMEM((3, LAYERS, *plane), f32),
             pltpu.VMEM((3, CHIPS, *plane), f32),
-            pltpu.VMEM((PARTS, CHIPS, SPAN, 4, *tile), f32),
-            pltpu.VMEM((PARTS, CHIPS, SPAN, 4, *tile), f32),
-            pltpu.VMEM((LAYERS, TILES, 4, *tile), f32),
+            pltpu.VMEM((PARTS, CHIPS, 4, *tile), f32),
+            pltpu.VMEM((PARTS, CHIPS, 4, *tile), f32),
+            pltpu.VMEM((LAYERS, 4, *plane), f32),
             pltpu.VMEM((LAYERS, 3, TILES, *tile), f32),
             pltpu.VMEM((LAYERS, 3, 3, TILES, *tile), f32),
             pltpu.VMEM((full, TILES, *tile), f32),
@@ -380,7 +400,7 @@
             pltpu.VMEM((3, full, TILES, *tile), f32),
             pltpu.VMEM((3, HALO, TILES, *tile), f32),
             pltpu.VMEM((3, HALO, TILES, *tile), f32),
-            dma((2,)), dma((2,)),
+            dma((2,)), dma((2, PARTS)),
             dma((1,)), dma((PARTS,)),
             dma((1,)), dma((CHIPS,)),
             dma((1,)), dma((CHIPS,)),

time: 45.2 us -> 43 us (0.951)
  Pallas kernels: 44 us -> 41.8 us
    pallas_call x1, Pallas kernels: 44 us -> 41.8 us  [per_device(): pl.pallas_call(kernel, out_shape=jax.ShapeDtypeStruct(velocity.shape[1:],...]
where the time goes in v3:
time: 43 us; the launch traced here: 42.7 us
  Pallas kernels  41.8 us (97%)
  local copies, waits for them, and re-layouts  0.88 us (2%)
    pallas_call x1, Pallas kernels, per_device(): pl.pallas_call(kernel, out_shape=jax.ShapeDtypeStruct(velocity.shape[1:],...  41.8 us
    unnamed x1, local copies, waits for them, and re-layouts  0.88 us

profile of v3, /device:TPU:1, one launch (start us, length us, event | category | flops | bytes accessed | tf_op | source)
XLA Modules:
  0.0 42.7 jit_solution(4831653188436449389)
XLA Ops:
  0.0 41.8 %shard_map.28 = f32[3,16,32,128]{3,2,1,0:T(8,128)S(1)} custom-call(f32[3,16,32,128]{3,2,1,0:T(8,128)} %bitcast.4, f32[3,16,32,128]{3,2,1,0:T(8,128)} %bitcast.5), custom_call_target="tpu_custom_call" | custom-call | tf_op jit(solution)/shard_map/pallas_call | solution.py:381
  41.8 0.9 %copy.4 = f32[1,3,16,32,128]{4,3,2,1,0:T(8,128)} copy(f32[1,3,16,32,128]{4,3,2,1,0:T(8,128)S(1)} %bitcast.3) | data formatting | bytes 1572864
